TPU v7x, 256 devices: a whole 4x4x8 slice. The times are simulated.
256 devices in a mesh: rep: 4 (over z_hi), fsdp: 64 (over y, z_lo, x, core).
Axes of the slice: x: 4, y: 4, z: 8 (z_hi: 4, z_lo: 2; z = z_hi * 2 + z_lo), core: 2. Of those that a mesh axis runs over, the one named last changes fastest.
Arguments:
- activations: bfloat16 [49152, 8192], P(('rep', 'fsdp')), may hold values from -6 to 6
- cotangent: bfloat16 [49152, 14336], P(('rep', 'fsdp')), may hold values from -0.109375 to 0.109375
- projector: bfloat16 [8192, 256], P('fsdp'), may hold values from -0.0625 to 0.0625
- moment1: float32 [256, 14336], P(None, 'fsdp'), may hold values from -4 to 4
- moment2: float32 [256, 14336], P(None, 'fsdp'), may hold values from 0.1 to 4
Outputs:
- moment1_new: float32 [256, 14336], P(None, 'fsdp')
- moment2_new: float32 [256, 14336], P(None, 'fsdp')
- update: bfloat16 [8192, 14336], P(None, 'fsdp')
All inputs are finite; a program needn't handle non-finite values.
Results may differ from a plain program's by a relative error of at most 0.0051.
Values may be sent and summed in bfloat16 or wider, within the bound.
A program may use at most 128 MiB of HBM per device.

v0:
```python
import jax
import jax.numpy as jnp
from jax import lax
from jax.sharding import PartitionSpec as P

STEP = 100


def adam_moments(grad, moment1, moment2):
    return (0.9 * moment1 + 0.1 * grad, 0.999 * moment2 + 0.001 * grad * grad)


def body(activations, cotangent, projector, moment1, moment2):
    low = jnp.dot(
        activations,
        lax.all_gather(projector, "fsdp", axis=0, tiled=True),
        preferred_element_type=jnp.float32,
    ).astype(jnp.bfloat16)
    group_grad = lax.psum_scatter(
        lax.dot_general(
            cotangent, low, (((0,), (0,)), ((), ())), preferred_element_type=jnp.float32
        ),
        "fsdp",
        scatter_dimension=0,
        tiled=True,
    ).T
    grad = lax.psum(group_grad, "rep")
    moment1_new, moment2_new = adam_moments(grad, moment1, moment2)
    first_fix = 1.0 - 0.9**STEP
    second_fix = 1.0 - 0.999**STEP
    direction = (moment1_new / first_fix / (jnp.sqrt(moment2_new / second_fix) + 1e-08)).astype(
        jnp.bfloat16
    )
    update = jnp.dot(
        lax.all_gather(projector, "fsdp", axis=0, tiled=True),
        direction,
        preferred_element_type=jnp.float32,
    )
    return (moment1_new, moment2_new, update.astype(jnp.bfloat16))


def solution(mesh):
    return jax.shard_map(
        body,
        mesh=mesh,
        in_specs=(
            P(("rep", "fsdp"), None),
            P(("rep", "fsdp"), None),
            P("fsdp", None),
            P(None, "fsdp"),
            P(None, "fsdp"),
        ),
        out_specs=(P(None, "fsdp"), P(None, "fsdp"), P(None, "fsdp")),
        check_vma=False,
    )
```

profile of v0, /device:TPU:2, one launch (start us, length us, event | category | flops | bytes accessed | tf_op | source)
XLA Modules:
  0.0 528.2 jit_solution(4577761439493059855)
XLA Ops:
  7.2 0.0 copy-start
  7.2 0.0 all-gather.2.cloned.1.call-start
  7.2 0.7 all-gather.2.cloned.1.call-update
  7.9 0.0 reduce-scatter.4.cloned.1.call-start
  8.0 111.9 %all-gather.2.cloned.1.call-done = bf16[8192,256]{1,0:T(8,128)(2,1)} async-done(((bf16[128,256]{1,0:T(8,128)(2,1)}), bf16[8192,256]{1,0:T(8,128)(2,1)}) %all-gather.2.cloned.1.call-update) | async-done | bytes 4194320 | tf_op jit(solution)/shard_map/all_gather | solution.py:16
  119.8 0.0 copy-done
  119.8 13.7 %convolution_bitcast_fusion = f32[14336,256]{0,1:T(8,128)} fusion(bf16[192,14336]{1,0:T(8,128)(2,1)} %param.6, bf16[192,8192]{1,0:T(8,128)(2,1)S(1)} %copy-done, bf16[8192,256]{1,0:T(8,128)(2,1)} %all-gather.2.cloned.1.call-done), kind=kOutput, calls=%fused_computation | convolution fusion | flops 2214641664 | bytes 27525120 | tf_op jit(solution)/shard_map/dot_general | solution.py:20
  133.5 15.2 %copy.16 = f32[14336,256]{1,0:T(8,128)} copy(f32[14336,256]{0,1:T(8,128)} %convolution_bitcast_fusion) | data formatting | bytes 29360128
  148.7 0.0 copy-start.1
  148.7 0.0 reduce-scatter.4.cloned.1.call-update
  148.7 0.0 all-reduce.2.cloned.1.call-start
  148.7 306.7 %reduce-scatter.4.cloned.1.call-done = f32[224,256]{1,0:T(8,128)} async-done(((f32[14336,256]{1,0:T(8,128)}), f32[224,256]{1,0:T(8,128)}) %reduce-scatter.4.cloned.1.call-update) | async-done | bytes 229392
  455.4 1.8 copy.17
  457.2 0.0 all-reduce.2.cloned.1.call-update
  457.2 0.0 copy-done.1
  457.2 0.8 copy.12
  458.1 1.8 copy.13
  459.9 51.7 %all-reduce.2.cloned.1.call-done = f32[256,224]{1,0:T(8,128)} async-done(((f32[256,224]{1,0:T(8,128)}), f32[256,224]{1,0:T(8,128)}) %all-reduce.2.cloned.1.call-update) | async-done | bytes 229392 | tf_op jit(solution)/shard_map/psum | solution.py:27
  511.5 1.9 fusion.1
  513.4 1.8 copy.14
  515.2 0.8 copy.15
  516.0 5.6 %fusion = bf16[8192,224]{0,1:T(8,128)(2,1)} fusion(bf16[8192,256]{1,0:T(8,128)(2,1)} %all-gather.2.cloned.1.call-done, f32[256,224]{1,0:T(8,128)S(1)} %get-tuple-element.9, f32[256,224]{1,0:T(8,128)} %get-tuple-element.10), kind=kOutput, calls=%fused_computation.2 | convolution fusion | flops 941645824 | bytes 8323072 | tf_op jit(solution)/shard_map/dot_general | solution.py:34
Async XLA Ops:
  7.2 112.7 %copy-start = (bf16[192,8192]{1,0:T(8,128)(2,1)S(1)}, bf16[192,8192]{1,0:T(8,128)(2,1)}, u32[]{:S(2)}) copy-start(bf16[192,8192]{1,0:T(8,128)(2,1)} %param.5) | copy-start | bytes 9437188
  7.2 112.6 %all-gather.2.cloned.1.call-start = ((), (), s32[]{:S(2)}) async-start(), calls=%async_computation.1 | async-start | bytes 4259840 | tf_op jit(solution)/shard_map/all_gather | solution.py:16
  7.9 447.5 %reduce-scatter.4.cloned.1.call-start = ((), (), s32[]{:S(2)}) async-start(), calls=%async_computation.3 | async-start | bytes 14909440
  148.7 308.6 %copy-start.1 = (f32[256,224]{0,1:T(8,128)S(1)}, f32[256,224]{0,1:T(8,128)}, u32[]{:S(2)}) copy-start(f32[256,224]{0,1:T(8,128)} %param.8) | copy-start | bytes 688132
  148.7 362.8 %all-reduce.2.cloned.1.call-start = ((), (), s32[]{:S(2)}) async-start(), calls=%async_computation.2 | async-start | bytes 524288 | tf_op jit(solution)/shard_map/psum | solution.py:27
Sparse Core Ops, SparseCore 0:
  9.8 109.9 all-gather.1
  148.8 306.5 reduce-scatter.3
  458.6 52.8 all-reduce.1
where the time goes:
time: 529 us; the launch traced here: 528 us
  waiting for transfers between devices  471 us (89%)
  local copies, waits for them, and re-layouts  22.1 us (4%)
  matrix products  19.3 us (4%)
  between operations  13.8 us (3%)
    unnamed x4, waiting for transfers between devices  307 us
    all_gather x1, waiting for transfers between devices, body(): lax.all_gather(projector, 'fsdp', axis=0, tiled=True)  112 us
    psum x1, waiting for transfers between devices, body(): grad = lax.psum(group_grad, 'rep')  51.7 us
    unnamed x10, local copies, waits for them, and re-layouts  22.1 us
    dot_general x1, matrix products, body(): lax.dot_general(cotangent, low, (((0,), (0,)), ((), ())), preferred_eleme...  13.7 us
  transfers between devices with their start and end apart: 3, of which 3 were waited for; matrix products, arithmetic and copies ran while one was open for 0% of the time, Pallas kernels for 0%

commit v1 on v0

--- a/solution.py
+++ b/solution.py
@@ -24,7 +24,7 @@
         scatter_dimension=0,
         tiled=True,
     ).T
-    grad = lax.psum(group_grad, "rep")
+    grad = jnp.sum(lax.all_gather(group_grad, "rep"), axis=0)
     moment1_new, moment2_new = adam_moments(grad, moment1, moment2)
     first_fix = 1.0 - 0.9**STEP
     second_fix = 1.0 - 0.999**STEP

time: 529 us -> 506 us (0.957); the launches traced: 528 us -> 497 us
  waiting for transfers between devices: 471 us -> 417 us
  blocking collectives: 0 us -> 19.5 us
    psum x1 -> x0, waiting for transfers between devices: 51.7 us -> none  [body(): grad = lax.psum(group_grad, 'rep')]
    all_gather x0 -> x1, blocking collectives: none -> 19.5 us  [body(): grad = jnp.sum(lax.all_gather(group_grad, 'rep'), axis=0)]
    unnamed x4 -> x3, waiting for transfers between devices: 307 us -> 306 us
  transfers between devices with their start and end apart: 3 -> 2, of which waited for: 3 -> 2; matrix products, arithmetic and copies ran while one was open for 0% -> 1% of each run, Pallas kernels for 0% -> 0%
where the time goes in v1:
time: 506 us; the launch traced here: 497 us
  waiting for transfers between devices  417 us (82%)
  local copies, waits for them, and re-layouts  22.3 us (4%)
  blocking collectives  19.5 us (4%)
  matrix products  19.3 us (4%)
  between operations  14.1 us (3%)
    unnamed x3, waiting for transfers between devices  306 us
    all_gather x1, waiting for transfers between devices, body(): lax.all_gather(projector, 'fsdp', axis=0, tiled=True)  112 us
    unnamed x10, local copies, waits for them, and re-layouts  22.3 us
    all_gather x1, blocking collectives, body(): grad = jnp.sum(lax.all_gather(group_grad, 'rep'), axis=0)  19.5 us
    dot_general x1, matrix products, body(): lax.dot_general(cotangent, low, (((0,), (0,)), ((), ())), preferred_eleme...  13.7 us
  transfers between devices with their start and end apart: 2, of which 2 were waited for; matrix products, arithmetic and copies ran while one was open for 1% of the time, Pallas kernels for 0%

profile of v1, /device:TPU:2, one launch (start us, length us, event | category | flops | bytes accessed | tf_op | source)
XLA Modules:
  0.0 496.7 jit_solution(2085593984659715943)
XLA Ops:
  7.2 0.0 copy-start
  7.2 0.0 all-gather.3.cloned.1.call-start
  7.2 0.7 all-gather.3.cloned.1.call-update
  7.9 0.0 reduce-scatter.4.cloned.1.call-start
  8.0 111.9 %all-gather.3.cloned.1.call-done = bf16[8192,256]{1,0:T(8,128)(2,1)} async-done(((bf16[128,256]{1,0:T(8,128)(2,1)}), bf16[8192,256]{1,0:T(8,128)(2,1)}) %all-gather.3.cloned.1.call-update) | async-done | bytes 4194320 | tf_op jit(solution)/shard_map/all_gather | solution.py:16
  119.8 0.0 copy-done
  119.8 13.7 %convolution_bitcast_fusion = f32[14336,256]{0,1:T(8,128)} fusion(bf16[192,14336]{1,0:T(8,128)(2,1)} %param.6, bf16[192,8192]{1,0:T(8,128)(2,1)S(1)} %copy-done, bf16[8192,256]{1,0:T(8,128)(2,1)} %all-gather.3.cloned.1.call-done), kind=kOutput, calls=%fused_computation | convolution fusion | flops 2214641664 | bytes 27525120 | tf_op jit(solution)/shard_map/dot_general | solution.py:20
  133.5 15.1 %copy.12 = f32[14336,256]{1,0:T(8,128)} copy(f32[14336,256]{0,1:T(8,128)} %convolution_bitcast_fusion) | data formatting | bytes 29360128
  148.7 0.0 copy-start.1
  148.7 0.0 reduce-scatter.4.cloned.1.call-update
  148.7 0.9 copy-done.1
  149.6 0.8 copy.8
  150.4 1.8 copy.9
  152.2 304.9 %reduce-scatter.4.cloned.1.call-done = f32[224,256]{1,0:T(8,128)} async-done(((f32[14336,256]{1,0:T(8,128)}), f32[224,256]{1,0:T(8,128)}) %reduce-scatter.4.cloned.1.call-update) | async-done | bytes 229392
  457.2 1.1 copy.13
  458.2 19.5 %all-gather = f32[1024,224]{1,0:T(8,128)} all-gather(f32[256,224]{1,0:T(8,128)S(1)} %bitcast.21), channel_id=2, replica_groups=mesh['rep'=4,'fsdp'=64] {'rep'}, dimensions={0}, use_global_device_ids=true | all-gather | bytes 1146880 | tf_op jit(solution)/shard_map/all_gather | solution.py:27
  477.8 2.0 reduce_sum.9
  479.8 1.9 fusion.1
  481.7 1.8 copy.10
  483.4 0.8 copy.11
  484.3 5.6 %fusion = bf16[8192,224]{0,1:T(8,128)(2,1)} fusion(bf16[8192,256]{1,0:T(8,128)(2,1)} %all-gather.3.cloned.1.call-done, f32[256,224]{1,0:T(8,128)S(1)} %get-tuple-element.6, f32[256,224]{1,0:T(8,128)} %get-tuple-element.7), kind=kOutput, calls=%fused_computation.2 | convolution fusion | flops 941645824 | bytes 8323072 | tf_op jit(solution)/shard_map/dot_general | solution.py:34
Async XLA Ops:
  7.2 112.7 %copy-start = (bf16[192,8192]{1,0:T(8,128)(2,1)S(1)}, bf16[192,8192]{1,0:T(8,128)(2,1)}, u32[]{:S(2)}) copy-start(bf16[192,8192]{1,0:T(8,128)(2,1)} %param.5) | copy-start | bytes 9437188
  7.2 112.6 %all-gather.3.cloned.1.call-start = ((), (), s32[]{:S(2)}) async-start(), calls=%async_computation.1 | async-start | bytes 4259840 | tf_op jit(solution)/shard_map/all_gather | solution.py:16
  7.9 449.2 %reduce-scatter.4.cloned.1.call-start = ((), (), s32[]{:S(2)}) async-start(), calls=%async_computation.2 | async-start | bytes 14909440
  148.7 0.9 copy-start.1
Sparse Core Ops, SparseCore 0:
  9.8 109.9 all-gather.2
  148.8 308.2 reduce-scatter.3

commit v2 on v0

--- a/solution.py
+++ b/solution.py
@@ -13,7 +13,9 @@
 def body(activations, cotangent, projector, moment1, moment2):
     low = jnp.dot(
         activations,
-        lax.all_gather(projector, "fsdp", axis=0, tiled=True),
+        jnp.concatenate(
+            lax.all_to_all(jnp.stack([projector] * lax.axis_size("fsdp")), "fsdp", 0, 0), axis=0
+        ),
         preferred_element_type=jnp.float32,
     ).astype(jnp.bfloat16)
     group_grad = lax.psum_scatter(

time: 529 us -> 583 us (1.10)
  blocking collectives: 0 us -> 60 us
  waiting for transfers between devices: 471 us -> 461 us
    all_to_all x0 -> x1, blocking collectives: none -> 60 us  [body(): lax.all_to_all(jnp.stack([projector] * lax.axis_size('fsdp')), 'fsdp', 0, 0)]
    all_gather x1, waiting for transfers between devices: 112 us -> 103 us  [body(): lax.all_gather(projector, 'fsdp', axis=0, tiled=True)]
  transfers between devices with their start and end apart: 3 -> 3, of which waited for: 3 -> 3; matrix products, arithmetic and copies ran while one was open for 0% -> 1% of each run, Pallas kernels for 0% -> 0%
where the time goes in v2:
time: 583 us; the launch traced here: 580 us
  waiting for transfers between devices  461 us (79%)
  blocking collectives  60 us (10%)
  local copies, waits for them, and re-layouts  23.6 us (4%)
  matrix products  19.4 us (3%)
  between operations  13.8 us (2%)
    unnamed x4, waiting for transfers between devices  308 us
    all_gather x1, waiting for transfers between devices, body(): lax.all_gather(projector, 'fsdp', axis=0, tiled=True)  103 us
    all_to_all x1, blocking collectives, body(): lax.all_to_all(jnp.stack([projector] * lax.axis_size('fsdp')), 'fsdp', 0, 0)  60 us
    psum x1, waiting for transfers between devices, body(): grad = lax.psum(group_grad, 'rep')  50.8 us
    unnamed x10, local copies, waits for them, and re-layouts  22.2 us
    dot_general x1, matrix products, body(): lax.dot_general(cotangent, low, (((0,), (0,)), ((), ())), preferred_eleme...  13.7 us
  transfers between devices with their start and end apart: 3, of which 3 were waited for; matrix products, arithmetic and copies ran while one was open for 1% of the time, Pallas kernels for 0%

profile of v2, /device:TPU:2, one launch (start us, length us, event | category | flops | bytes accessed | tf_op | source)
XLA Modules:
  0.0 580.2 jit_solution(9406236051628088035)
XLA Ops:
  7.2 0.0 copy-start
  7.2 0.0 reduce-scatter.4.cloned.1.call-start
  7.2 1.5 stack.2
  8.7 60.0 %all_to_all.5 = bf16[64,128,256]{2,1,0:T(8,128)(2,1)} all-to-all(bf16[64,128,256]{2,1,0:T(8,128)(2,1)S(1)} %stack.2), channel_id=1, replica_groups=mesh['rep'=4,'fsdp'=64] {'fsdp'}, dimensions={0} | all-to-all | bytes 8388608 | tf_op jit(solution)/shard_map/all_to_all | solution.py:17
  68.7 0.0 copy-done
  68.7 13.7 %convolution_bitcast_fusion = f32[14336,256]{0,1:T(8,128)} fusion(bf16[192,14336]{1,0:T(8,128)(2,1)} %param.6, bf16[192,8192]{1,0:T(8,128)(2,1)S(1)} %copy-done, bf16[8192,256]{1,0:T(8,128)(2,1)} %bitcast.20), kind=kOutput, calls=%fused_computation | convolution fusion | flops 2214641664 | bytes 27525120 | tf_op jit(solution)/shard_map/dot_general | solution.py:22
  82.5 15.1 %copy.16 = f32[14336,256]{1,0:T(8,128)} copy(f32[14336,256]{0,1:T(8,128)} %convolution_bitcast_fusion) | data formatting | bytes 29360128
  97.6 0.0 copy-start.1
  97.6 0.0 reduce-scatter.4.cloned.1.call-update
  97.6 0.0 all-reduce.2.cloned.1.call-start
  97.7 306.8 %reduce-scatter.4.cloned.1.call-done = f32[224,256]{1,0:T(8,128)} async-done(((f32[14336,256]{1,0:T(8,128)}), f32[224,256]{1,0:T(8,128)}) %reduce-scatter.4.cloned.1.call-update) | async-done | bytes 229392
  404.5 1.8 copy.17
  406.2 0.0 all-reduce.2.cloned.1.call-update
  406.3 0.0 all-gather.2.cloned.1.call-start
  406.3 0.7 all-gather.2.cloned.1.call-update
  407.0 0.0 copy-done.1
  407.0 0.9 copy.12
  407.9 1.8 copy.13
  409.7 50.8 %all-reduce.2.cloned.1.call-done = f32[256,224]{1,0:T(8,128)} async-done(((f32[256,224]{1,0:T(8,128)}), f32[256,224]{1,0:T(8,128)}) %all-reduce.2.cloned.1.call-update) | async-done | bytes 229392 | tf_op jit(solution)/shard_map/psum | solution.py:29
  460.5 1.9 fusion.1
  462.4 1.8 copy.14
  464.2 0.8 copy.15
  465.0 103.1 %all-gather.2.cloned.1.call-done = bf16[8192,256]{1,0:T(8,128)(2,1)} async-done(((bf16[128,256]{1,0:T(8,128)(2,1)}), bf16[8192,256]{1,0:T(8,128)(2,1)}) %all-gather.2.cloned.1.call-update) | async-done | bytes 4194320 | tf_op jit(solution)/shard_map/all_gather | solution.py:37
  568.1 5.6 fusion
Async XLA Ops:
  7.2 61.6 %copy-start = (bf16[192,8192]{1,0:T(8,128)(2,1)S(1)}, bf16[192,8192]{1,0:T(8,128)(2,1)}, u32[]{:S(2)}) copy-start(bf16[192,8192]{1,0:T(8,128)(2,1)} %param.5) | copy-start | bytes 9437188
  7.2 397.3 %reduce-scatter.4.cloned.1.call-start = ((), (), s32[]{:S(2)}) async-start(), calls=%async_computation.4 | async-start | bytes 14909440
  97.6 309.4 %copy-start.1 = (f32[256,224]{0,1:T(8,128)S(1)}, f32[256,224]{0,1:T(8,128)}, u32[]{:S(2)}) copy-start(f32[256,224]{0,1:T(8,128)} %param.8) | copy-start | bytes 688132
  97.6 362.9 %all-reduce.2.cloned.1.call-start = ((), (), s32[]{:S(2)}) async-start(), calls=%async_computation.2 | async-start | bytes 524288 | tf_op jit(solution)/shard_map/psum | solution.py:29
  406.3 161.8 %all-gather.2.cloned.1.call-start = ((), (), s32[]{:S(2)}) async-start(), calls=%async_computation.3 | async-start | bytes 4259840 | tf_op jit(solution)/shard_map/all_gather | solution.py:37
Sparse Core Ops, SparseCore 0:
  97.8 306.6 reduce-scatter.3
  407.7 52.8 all-reduce.1
  462.4 105.6 all-gather.1
